TPU v7x, 512 devices: a whole 4x4x16 slice. The times are simulated.
512 devices in a mesh: grp: 4 (over x_lo, core), dp: 32 (over z, x_hi), mp: 4 (over y).
Axes of the slice: x: 4 (x_hi: 2, x_lo: 2; x = x_hi * 2 + x_lo), y: 4, z: 16, core: 2. Of those that a mesh axis runs over, the one named last changes fastest.
Arguments:
- neighbours: bfloat16 [512, 256, 896], P(('grp', 'dp')), may hold values from -6 to 6
- counts: int32 [512], P(('grp', 'dp')), may hold values from 0 to 2
- owner: int32 [512], P(('grp', 'dp')), may hold values from 0 to 511, as said below
- norm_gain: float32 [896], replicated, may hold values from 0.1 to 1.9
- w_in: bfloat16 [896, 3584], P('dp', 'mp'), may hold values from -0.1875 to 0.1875
- w_out: bfloat16 [3584, 896], P('mp', 'dp'), may hold values from -0.09375 to 0.09375
- w_key: bfloat16 [896, 4096], P('dp', 'mp'), may hold values from -0.1875 to 0.1875
- w_value: bfloat16 [896, 4096], P('dp', 'mp'), may hold values from -0.1875 to 0.1875
- queries: bfloat16 [32768, 4096], P(('grp', 'dp'), 'mp'), may hold values from -150 to 150
Outputs:
- attended: bfloat16 [32768, 4096], P(('grp', 'dp'), 'mp')
Inputs may be any that keep to these rules, and one draw needn't show every extreme that they name: owner is a permutation of the 512 query blocks. Span c stands on device c // 4 of grp+dp (index grp * 32 + dp); block owner[c] lies on device owner[c] // 4, which has the same dp index. Each device keeps 2 of its spans (their blocks lie on the device itself) and sends the other 2 to one other device along grp.
All inputs are finite; a program needn't handle non-finite values.
Results may differ from a plain program's by a relative error of at most 0.02.
Values may be sent and summed in bfloat16 or wider, within the bound.
A program may use at most 64 MiB of HBM per device.

v0:
```python
import jax
import jax.numpy as jnp
from jax import lax
from jax.sharding import PartitionSpec as P

HEAD = 128
NLEN = 128


def place_rows(received, meta, span_count):
    targets = jnp.arange(span_count, dtype=jnp.int32)[:, None]
    picker = meta[:, 0][None, :] == targets
    placed = jnp.einsum(
        "jb,btc->jtc", picker.astype(jnp.bfloat16), received, preferred_element_type=jnp.float32
    ).astype(jnp.bfloat16)
    live_counts = jnp.sum(jnp.where(picker, meta[:, 1][None, :], 0), axis=1).astype(jnp.int32)
    return (placed, live_counts)


def route_table(dest_grp, dest_slot, valid, extra, group_count, capacity):
    entries = dest_grp.shape[0]
    order = jnp.arange(entries, dtype=jnp.int32)
    earlier = (
        valid[None, :]
        & (dest_grp[None, :] == dest_grp[:, None])
        & (order[None, :] < order[:, None])
    )
    rank = jnp.sum(earlier.astype(jnp.int32), axis=1)
    bucket = jnp.where(valid, dest_grp * capacity + rank, -1)
    picker = bucket[None, :] == jnp.arange(group_count * capacity, dtype=jnp.int32)[:, None]
    slot_sent = jnp.sum(jnp.where(picker, dest_slot[None, :] + 1, 0), axis=1) - 1
    extra_sent = jnp.sum(jnp.where(picker, extra[None, :], 0), axis=1)
    meta = jnp.stack([slot_sent, extra_sent], axis=1)
    return (picker, meta)


def bucket_rows(rows, owner, extra, group_count, dp_count):
    span_count = owner.shape[0]
    dest_grp = owner // span_count // dp_count
    dest_slot = owner % span_count
    valid = jnp.ones((span_count,), dtype=bool)
    picker, meta = route_table(dest_grp, dest_slot, valid, extra, group_count, span_count // 2)
    packed = jnp.einsum(
        "bj,jtc->btc", picker.astype(jnp.bfloat16), rows, preferred_element_type=jnp.float32
    ).astype(jnp.bfloat16)
    return (packed, meta)


def attend_local(query_blocks, keys, values, live_counts):
    key_len = keys.shape[1]
    scores = jnp.einsum(
        "cqhd,ckhd->chqk", query_blocks, keys, preferred_element_type=jnp.float32
    ) * HEAD ** (-0.5)
    position = jnp.arange(key_len, dtype=jnp.int32) // NLEN
    live = (position[None, :] < live_counts[:, None])[:, None, None, :]
    masked = jnp.where(live, scores, -1e30)
    top = jnp.maximum(jnp.max(masked, axis=-1), 0.0)
    probs = jnp.where(live, jnp.exp(masked - top[..., None]), 0.0)
    denom = jnp.sum(probs, axis=-1) + jnp.exp(-top)
    weights = probs.astype(jnp.bfloat16)
    mixed = jnp.einsum("chqk,ckhd->cqhd", weights, values, preferred_element_type=jnp.float32)
    mixed = mixed / jnp.transpose(denom, (0, 2, 1))[..., None]
    span_count, span_len = (mixed.shape[0], mixed.shape[1])
    return mixed.astype(jnp.bfloat16).reshape(span_count, span_len, -1)


def on_device(neighbours, counts, owner, norm_gain, w_in, w_out, w_key, w_value, queries):
    span_count, key_len, enc_width = neighbours.shape
    group_count = lax.axis_size("grp")
    dp_count = lax.axis_size("dp")
    local_width = queries.shape[1]
    query_rows = queries.reshape(span_count, -1, local_width)
    flat = neighbours.astype(jnp.float32).reshape(-1, enc_width)
    meansq = jnp.mean(flat * flat, axis=-1, keepdims=True)
    normed = (flat * lax.rsqrt(meansq + 1e-06) * norm_gain).astype(jnp.bfloat16)
    columns = normed
    pre = jnp.dot(
        columns, lax.all_gather(w_in, "dp", axis=0, tiled=True), preferred_element_type=jnp.float32
    )
    hidden = jax.nn.gelu(pre, approximate=False).astype(jnp.bfloat16)
    partial_out = jnp.dot(
        hidden, lax.all_gather(w_out, "dp", axis=1, tiled=True), preferred_element_type=jnp.float32
    )
    total = lax.psum(partial_out, "mp")
    states = (flat + total).astype(jnp.bfloat16).reshape(span_count, key_len, enc_width)
    packed, meta = bucket_rows(states, owner, counts, group_count, dp_count)
    received, received_meta = (
        lax.all_to_all(packed, "grp", split_axis=0, concat_axis=0, tiled=True),
        lax.all_to_all(meta, "grp", split_axis=0, concat_axis=0, tiled=True),
    )
    served, live_counts = place_rows(received, received_meta, span_count)
    served_flat = served.reshape(-1, enc_width)
    columns = served_flat
    key_total = jnp.dot(
        columns, lax.all_gather(w_key, "dp", axis=0, tiled=True), preferred_element_type=jnp.float32
    )
    value_total = jnp.dot(
        columns,
        lax.all_gather(w_value, "dp", axis=0, tiled=True),
        preferred_element_type=jnp.float32,
    )
    heads = w_key.shape[1] // HEAD
    keys = key_total.astype(jnp.bfloat16).reshape(span_count, key_len, heads, HEAD)
    values = value_total.astype(jnp.bfloat16).reshape(span_count, key_len, heads, HEAD)
    query_blocks = query_rows.reshape(span_count, -1, heads, HEAD)
    mixed = attend_local(query_blocks, keys, values, live_counts)
    return mixed.reshape(queries.shape[0], queries.shape[1])


def solution(mesh):
    placed = (
        P(("grp", "dp"), None, None),
        P(("grp", "dp")),
        P(("grp", "dp")),
        P(),
        P("dp", "mp"),
        P("mp", "dp"),
        P("dp", "mp"),
        P("dp", "mp"),
        P(("grp", "dp"), "mp"),
    )
    return jax.shard_map(
        on_device, mesh=mesh, in_specs=placed, out_specs=P(("grp", "dp"), "mp"), check_vma=False
    )
```

profile of v0, /device:TPU:8, one launch (start us, length us, event | category | flops | bytes accessed | tf_op | source)
XLA Modules:
  0.0 746.3 jit_solution(8559613204974902349)
XLA Ops:
  8.1 1.9 fusion.3
  10.0 2.0 fusion.5
  12.0 150.9 %all-gather.11.cloned.1.call-done = bf16[32,28,896]{2,1,0:T(8,128)(2,1)} async-done(((bf16[1,28,896]{2,1,0:T(8,128)(2,1)}), bf16[32,28,896]{2,1,0:T(8,128)(2,1)}) %all-gather.11.cloned.1.call-update) | async-done | bytes 1605648 | tf_op jit(solution)/shard_map/all_gather | solution.py:82
  162.9 2.4 reshape.107
  165.3 143.2 %all-gather.9.cloned.1.call-done = bf16[32,28,896]{2,1,0:T(8,128)(2,1)} async-done(((bf16[1,28,896]{2,1,0:T(8,128)(2,1)}), bf16[32,28,896]{2,1,0:T(8,128)(2,1)}) %all-gather.9.cloned.1.call-update) | async-done | bytes 1605648 | tf_op jit(solution)/shard_map/all_gather | solution.py:78
  308.5 3.5 reshape.105
  312.0 14.2 %fusion.23 = f32[1024,896]{1,0:T(8,128)} fusion(bf16[896,896]{1,0:T(8,128)(2,1)S(1)} %reshape.107, bf16[1024,896]{1,0:T(8,128)(2,1)S(1)} %fusion.5, bf16[896,896]{1,0:T(8,128)(2,1)} %reshape.105), kind=kOutput, calls=%fused_computation.41 | convolution fusion | flops 3347972096 | bytes 8716288 | tf_op jit(solution)/shard_map/dot_general | solution.py:81
  328.6 3.4 all-to-all-start
  332.0 87.4 %all-reduce.2.cloned.1.call-done = f32[1024,896]{1,0:T(8,128)} async-done(((f32[1024,896]{1,0:T(8,128)}), f32[1024,896]{1,0:T(8,128)}) %all-reduce.2.cloned.1.call-update) | async-done | bytes 3670032 | tf_op jit(solution)/shard_map/psum | solution.py:84
  419.4 2.4 fusion.6
  421.8 2.8 convolution_convert_fusion
  424.6 2.4 copy.31
  427.0 4.9 all-to-all-start.1
  432.3 141.0 %all-gather.13.cloned.1.call-done = bf16[32,28,1024]{2,1,0:T(8,128)(2,1)} async-done(((bf16[1,28,1024]{2,1,0:T(8,128)(2,1)}), bf16[32,28,1024]{2,1,0:T(8,128)(2,1)}) %all-gather.13.cloned.1.call-update) | async-done | bytes 1835024 | tf_op jit(solution)/shard_map/all_gather | solution.py:99
  573.3 2.5 reshape.109
  575.8 144.5 %all-gather.15.cloned.1.call-done = bf16[32,28,1024]{2,1,0:T(8,128)(2,1)} async-done(((bf16[1,28,1024]{2,1,0:T(8,128)(2,1)}), bf16[32,28,1024]{2,1,0:T(8,128)(2,1)}) %all-gather.15.cloned.1.call-update) | async-done | bytes 1835024 | tf_op jit(solution)/shard_map/all_gather | solution.py:95
  720.3 3.7 reshape.111
  724.1 4.5 fusion.25
  728.8 2.4 convert_bitcast_fusion.1
  732.6 2.3 convert_bitcast_fusion
  735.6 0.9 bitcast_reduce_fusion
  736.5 0.9 fusion.28
  737.5 1.0 fusion.36
  738.8 0.9 copy.66
  (46 shorter events, 6.8 us)
Async XLA Ops:
  6.5 156.4 %all-gather.11.cloned.1.call-start = ((), (), s32[]{:S(2)}) async-start(), calls=%async_computation.4 | async-start | bytes 1892352 | tf_op jit(solution)/shard_map/all_gather | solution.py:82
  7.3 301.2 %all-gather.9.cloned.1.call-start = ((), (), s32[]{:S(2)}) async-start(), calls=%async_computation.3 | async-start | bytes 1892352 | tf_op jit(solution)/shard_map/all_gather | solution.py:78
  8.0 411.4 %all-reduce.2.cloned.1.call-start = ((), (), s32[]{:S(2)}) async-start(), calls=%async_computation.2 | async-start | bytes 7340032 | tf_op jit(solution)/shard_map/psum | solution.py:84
  326.3 1.2 copy-start.4
  326.3 1.4 copy-start.3
  326.3 93.1 %copy-start = (bf16[4,256,896]{2,1,0:T(8,128)(2,1)S(1)}, bf16[4,256,896]{2,1,0:T(8,128)(2,1)}, u32[]{:S(2)}) copy-start(bf16[4,256,896]{2,1,0:T(8,128)(2,1)} %param.9) | copy-start | bytes 5505028
  326.3 247.1 %all-gather.13.cloned.1.call-start = ((), (), s32[]{:S(2)}) async-start(), calls=%async_computation.5 | async-start | bytes 2162688 | tf_op jit(solution)/shard_map/all_gather | solution.py:99
  326.9 393.5 %all-gather.15.cloned.1.call-start = ((), (), s32[]{:S(2)}) async-start(), calls=%async_computation.6 | async-start | bytes 2162688 | tf_op jit(solution)/shard_map/all_gather | solution.py:95
  328.6 98.5 %all-to-all-start = ((s32[4,2,2]{1,2,0:T(2,128)}), s32[4,2,2]{1,2,0:T(2,128)S(1)}, u32[]{:S(2)}, u32[]{:S(2)}) async-start(s32[4,2,2]{1,2,0:T(2,128)} %copy.28), calls=%async_computation | async-start | bytes 8192 | tf_op jit(solution)/shard_map/all_to_all | solution.py:89
  427.0 4.9 copy-start.2
  427.0 297.0 %all-to-all-start.1 = ((bf16[8,256,896]{2,1,0:T(8,128)(2,1)}), bf16[8,256,896]{2,1,0:T(8,128)(2,1)}, u32[]{:S(2)}, u32[]{:S(2)}) async-start(bf16[8,256,896]{2,1,0:T(8,128)(2,1)} %copy.31), calls=%async_computation.1 | async-start | bytes 7340032 | tf_op jit(solution)/shard_map/all_to_all | solution.py:88
  731.1 1.5 copy-start.1
Sparse Core Ops, SparseCore 0:
  10.4 152.4 all-gather.10
  166.0 142.4 all-gather.8
  326.4 92.9 all-reduce.1
  422.3 150.9 all-gather.12
  576.3 144.0 all-gather.14
where the time goes:
time: 747 us; the launch traced here: 746 us
  waiting for transfers between devices  669 us (90%)
  matrix products  28.1 us (4%)
  local copies, waits for them, and re-layouts  19.1 us (3%)
  between operations  13.4 us (2%)
  starting transfers between devices  8.46 us (1%)
  other arithmetic  7.76 us (1%)
    all_gather x1, waiting for transfers between devices, on_device(): lax.all_gather(w_out, 'dp', axis=1, tiled=True)  151 us
    all_gather x1, waiting for transfers between devices, on_device(): lax.all_gather(w_key, 'dp', axis=0, tiled=True)  145 us
    all_gather x1, waiting for transfers between devices, on_device(): lax.all_gather(w_in, 'dp', axis=0, tiled=True)  143 us
    all_gather x1, waiting for transfers between devices, on_device(): lax.all_gather(w_value, 'dp', axis=0, tiled=True)  141 us
    psum x1, waiting for transfers between devices, on_device(): total = lax.psum(partial_out, 'mp')  87.4 us
    unnamed x19, local copies, waits for them, and re-layouts  15.3 us
  transfers between devices with their start and end apart: 7, of which 5 were waited for; matrix products, arithmetic and copies ran while one was open for 3% of the time, Pallas kernels for 0%

commit v1 on v0

--- a/solution.py
+++ b/solution.py
@@ -81,7 +81,8 @@
     partial_out = jnp.dot(
         hidden, lax.all_gather(w_out, "dp", axis=1, tiled=True), preferred_element_type=jnp.float32
     )
-    total = lax.psum(partial_out, "mp")
+    pieces = lax.all_gather(partial_out, "mp")
+    total = jnp.sum(pieces, axis=0)
     states = (flat + total).astype(jnp.bfloat16).reshape(span_count, key_len, enc_width)
     packed, meta = bucket_rows(states, owner, counts, group_count, dp_count)
     received, received_meta = (

time: 747 us -> 792 us (1.060)
  waiting for transfers between devices: 669 us -> 707 us
  other arithmetic: 7.76 us -> 16.1 us
    all_gather x0 -> x1, waiting for transfers between devices: none -> 133 us  [on_device(): pieces = lax.all_gather(partial_out, 'mp')]
    psum x1 -> x0, waiting for transfers between devices: 87.4 us -> none  [on_device(): total = lax.psum(partial_out, 'mp')]
    all_gather x1, waiting for transfers between devices: 141 us -> 133 us  [on_device(): lax.all_gather(w_value, 'dp', axis=0, tiled=True)]
    reduce_sum x0 -> x1, other arithmetic: none -> 8.28 us  [on_device(): total = jnp.sum(pieces, axis=0)]
  transfers between devices with their start and end apart: 7 -> 7, of which waited for: 5 -> 5; matrix products, arithmetic and copies ran while one was open for 3% -> 4% of each run, Pallas kernels for 0% -> 0%
where the time goes in v1:
time: 792 us
  waiting for transfers between devices  707 us (89%)
  matrix products  28.1 us (4%)
  local copies, waits for them, and re-layouts  19.2 us (2%)
  other arithmetic  16.1 us (2%)
  between operations  13.4 us (2%)
  starting transfers between devices  8.46 us (1%)
    all_gather x1, waiting for transfers between devices, on_device(): lax.all_gather(w_out, 'dp', axis=1, tiled=True)  151 us
    all_gather x1, waiting for transfers between devices, on_device(): lax.all_gather(w_key, 'dp', axis=0, tiled=True)  145 us
    all_gather x1, waiting for transfers between devices, on_device(): lax.all_gather(w_in, 'dp', axis=0, tiled=True)  143 us
    all_gather x1, waiting for transfers between devices, on_device(): pieces = lax.all_gather(partial_out, 'mp')  133 us
    all_gather x1, waiting for transfers between devices, on_device(): lax.all_gather(w_value, 'dp', axis=0, tiled=True)  133 us
  transfers between devices with their start and end apart: 7, of which 5 were waited for; matrix products, arithmetic and copies ran while one was open for 4% of the time, Pallas kernels for 0%

profile of v1, /device:TPU:8, one launch (start us, length us, event | category | flops | bytes accessed | tf_op | source)
XLA Modules:
  0.0 791.8 jit_solution(14676164460622676423)
XLA Ops:
  8.1 1.9 multiply_reduce_fusion
  10.0 2.0 fusion.4
  12.0 150.9 %all-gather.15.cloned.1.call-done = bf16[32,28,896]{2,1,0:T(8,128)(2,1)} async-done(((bf16[1,28,896]{2,1,0:T(8,128)(2,1)}), bf16[32,28,896]{2,1,0:T(8,128)(2,1)}) %all-gather.15.cloned.1.call-update) | async-done | bytes 1605648 | tf_op jit(solution)/shard_map/all_gather | solution.py:82
  162.9 2.4 reshape.106
  165.3 143.2 %all-gather.13.cloned.1.call-done = bf16[32,28,896]{2,1,0:T(8,128)(2,1)} async-done(((bf16[1,28,896]{2,1,0:T(8,128)(2,1)}), bf16[32,28,896]{2,1,0:T(8,128)(2,1)}) %all-gather.13.cloned.1.call-update) | async-done | bytes 1605648 | tf_op jit(solution)/shard_map/all_gather | solution.py:78
  308.5 3.6 reshape.104
  312.1 14.2 %fusion.21 = f32[1024,896]{1,0:T(8,128)} fusion(bf16[896,896]{1,0:T(8,128)(2,1)S(1)} %reshape.106, bf16[1024,896]{1,0:T(8,128)(2,1)S(1)} %fusion.4, bf16[896,896]{1,0:T(8,128)(2,1)} %reshape.104), kind=kOutput, calls=%fused_computation.39 | convolution fusion | flops 3347972096 | bytes 8716288 | tf_op jit(solution)/shard_map/dot_general | solution.py:81
  328.6 3.4 all-to-all-start
  332.0 132.8 %all-gather.11.cloned.1.call-done = f32[4096,896]{1,0:T(8,128)} async-done(((f32[1024,896]{1,0:T(8,128)}), f32[4096,896]{1,0:T(8,128)}) %all-gather.11.cloned.1.call-update) | async-done | bytes 14680080 | tf_op jit(solution)/shard_map/all_gather | solution.py:84
  464.8 8.3 %reduce_sum.69 = f32[1024,896]{1,0:T(8,128)} reduce(f32[4,1024,896]{2,1,0:T(8,128)} %bitcast.73, f32[]{:T(128)} %constant.38.clone.1), dimensions={0}, to_apply=%region_4.5 | reduce | flops 2752512 | bytes 18350084 | tf_op jit(solution)/shard_map/reduce_sum | solution.py:85
  473.1 2.4 add_convert_fusion
  475.5 2.8 convolution_convert_fusion
  478.3 2.4 copy.31
  480.8 4.9 all-to-all-start.1
  486.1 132.7 %all-gather.17.cloned.1.call-done = bf16[32,28,1024]{2,1,0:T(8,128)(2,1)} async-done(((bf16[1,28,1024]{2,1,0:T(8,128)(2,1)}), bf16[32,28,1024]{2,1,0:T(8,128)(2,1)}) %all-gather.17.cloned.1.call-update) | async-done | bytes 1835024 | tf_op jit(solution)/shard_map/all_gather | solution.py:100
  618.8 2.5 reshape.108
  621.3 144.5 %all-gather.19.cloned.1.call-done = bf16[32,28,1024]{2,1,0:T(8,128)(2,1)} async-done(((bf16[1,28,1024]{2,1,0:T(8,128)(2,1)}), bf16[32,28,1024]{2,1,0:T(8,128)(2,1)}) %all-gather.19.cloned.1.call-update) | async-done | bytes 1835024 | tf_op jit(solution)/shard_map/all_gather | solution.py:96
  765.8 3.8 reshape.110
  769.6 4.5 fusion.23
  774.3 2.4 convert_bitcast_fusion.1
  778.1 2.3 convert_bitcast_fusion
  781.1 0.9 bitcast_reduce_fusion
  782.0 0.9 fusion.26
  783.0 1.0 fusion.34
  (47 shorter events, 7.7 us)
Async XLA Ops:
  6.5 156.4 %all-gather.15.cloned.1.call-start = ((), (), s32[]{:S(2)}) async-start(), calls=%async_computation.4 | async-start | bytes 1892352 | tf_op jit(solution)/shard_map/all_gather | solution.py:82
  7.3 301.2 %all-gather.13.cloned.1.call-start = ((), (), s32[]{:S(2)}) async-start(), calls=%async_computation.3 | async-start | bytes 1892352 | tf_op jit(solution)/shard_map/all_gather | solution.py:78
  8.0 456.8 %all-gather.11.cloned.1.call-start = ((), (), s32[]{:S(2)}) async-start(), calls=%async_computation.2 | async-start | bytes 18350080 | tf_op jit(solution)/shard_map/all_gather | solution.py:84
  326.3 1.2 copy-start.4
  326.3 1.4 copy-start.3
  326.3 292.5 %all-gather.17.cloned.1.call-start = ((), (), s32[]{:S(2)}) async-start(), calls=%async_computation.5 | async-start | bytes 2162688 | tf_op jit(solution)/shard_map/all_gather | solution.py:100
  326.9 438.9 %all-gather.19.cloned.1.call-start = ((), (), s32[]{:S(2)}) async-start(), calls=%async_computation.6 | async-start | bytes 2162688 | tf_op jit(solution)/shard_map/all_gather | solution.py:96
  328.6 152.2 %all-to-all-start = ((s32[4,2,2]{1,2,0:T(2,128)}), s32[4,2,2]{1,2,0:T(2,128)S(1)}, u32[]{:S(2)}, u32[]{:S(2)}) async-start(s32[4,2,2]{1,2,0:T(2,128)} %copy.28), calls=%async_computation | async-start | bytes 8192 | tf_op jit(solution)/shard_map/all_to_all | solution.py:90
  464.8 8.3 %copy-start = (bf16[4,256,896]{2,1,0:T(8,128)(2,1)S(1)}, bf16[4,256,896]{2,1,0:T(8,128)(2,1)}, u32[]{:S(2)}) copy-start(bf16[4,256,896]{2,1,0:T(8,128)(2,1)} %param.9) | copy-start | bytes 5505028
  480.8 4.9 copy-start.2
  480.8 288.8 %all-to-all-start.1 = ((bf16[8,256,896]{2,1,0:T(8,128)(2,1)}), bf16[8,256,896]{2,1,0:T(8,128)(2,1)}, u32[]{:S(2)}, u32[]{:S(2)}) async-start(bf16[8,256,896]{2,1,0:T(8,128)(2,1)} %copy.31), calls=%async_computation.1 | async-start | bytes 7340032 | tf_op jit(solution)/shard_map/all_to_all | solution.py:89
  776.6 1.5 copy-start.1
Sparse Core Ops, SparseCore 0:
  10.4 152.4 all-gather.14
  166.0 142.4 all-gather.12
  326.5 138.3 all-gather.10
  467.8 150.9 all-gather.16
  621.8 144.0 all-gather.18

commit v2 on v0

--- a/solution.py
+++ b/solution.py
@@ -65,6 +65,16 @@
 
 
 def on_device(neighbours, counts, owner, norm_gain, w_in, w_out, w_key, w_value, queries):
+
+    def point_forms(raw, at_axis):
+        v_now = lax.all_to_all(
+            jnp.stack(tuple((raw for _ in range(lax.axis_size("dp"))))),
+            "dp",
+            split_axis=0,
+            concat_axis=0,
+        )
+        return jnp.concatenate(v_now, axis=at_axis)
+
     span_count, key_len, enc_width = neighbours.shape
     group_count = lax.axis_size("grp")
     dp_count = lax.axis_size("dp")
@@ -78,9 +88,7 @@
         columns, lax.all_gather(w_in, "dp", axis=0, tiled=True), preferred_element_type=jnp.float32
     )
     hidden = jax.nn.gelu(pre, approximate=False).astype(jnp.bfloat16)
-    partial_out = jnp.dot(
-        hidden, lax.all_gather(w_out, "dp", axis=1, tiled=True), preferred_element_type=jnp.float32
-    )
+    partial_out = jnp.dot(hidden, point_forms(w_out, 1), preferred_element_type=jnp.float32)
     total = lax.psum(partial_out, "mp")
     states = (flat + total).astype(jnp.bfloat16).reshape(span_count, key_len, enc_width)
     packed, meta = bucket_rows(states, owner, counts, group_count, dp_count)

time: 747 us -> 634 us (0.85)
  waiting for transfers between devices: 669 us -> 537 us
  starting transfers between devices: 8.46 us -> 26.5 us
    all_gather x1 -> x0, waiting for transfers between devices: 151 us -> none  [on_device(): lax.all_gather(w_out, 'dp', axis=1, tiled=True)]
    all_gather x1, waiting for transfers between devices: 143 us -> 163 us  [on_device(): lax.all_gather(w_in, 'dp', axis=0, tiled=True)]
    all_to_all x0 -> x1, starting transfers between devices: none -> 18.1 us  [point_forms(): lax.all_to_all(jnp.stack(tuple((raw for _ in range(lax.axis_size('dp'))))...]
    unnamed x19 -> x22, local copies, waits for them, and re-layouts: 15.3 us -> 13 us
  transfers between devices with their start and end apart: 7 -> 7, of which waited for: 5 -> 4; matrix products, arithmetic and copies ran while one was open for 3% -> 3% of each run, Pallas kernels for 0% -> 0%
where the time goes in v2:
time: 634 us
  waiting for transfers between devices  537 us (85%)
  matrix products  28.2 us (4%)
  starting transfers between devices  26.5 us (4%)
  local copies, waits for them, and re-layouts  22.8 us (4%)
  between operations  13.4 us (2%)
    all_gather x1, waiting for transfers between devices, on_device(): lax.all_gather(w_in, 'dp', axis=0, tiled=True)  163 us
    all_gather x1, waiting for transfers between devices, on_device(): lax.all_gather(w_key, 'dp', axis=0, tiled=True)  143 us
    all_gather x1, waiting for transfers between devices, on_device(): lax.all_gather(w_value, 'dp', axis=0, tiled=True)  141 us
    psum x1, waiting for transfers between devices, on_device(): total = lax.psum(partial_out, 'mp')  87.4 us
    all_to_all x1, starting transfers between devices, point_forms(): lax.all_to_all(jnp.stack(tuple((raw for _ in range(lax.axis_size('dp'))))...  18.1 us
    dot_general x1, matrix products, on_device(): jnp.dot(hidden, point_forms(w_out, 1), preferred_element_type=jnp.float32)  14.2 us
    unnamed x22, local copies, waits for them, and re-layouts  13 us
  transfers between devices with their start and end apart: 7, of which 4 were waited for; matrix products, arithmetic and copies ran while one was open for 3% of the time, Pallas kernels for 0%

profile of v2, /device:TPU:8, one launch (start us, length us, event | category | flops | bytes accessed | tf_op | source)
XLA Modules:
  0.0 633.5 jit_solution(12620977055046838769)
XLA Ops:
  6.5 2.3 stack.8
  8.9 18.1 %all-to-all-start.1 = ((bf16[32,896,28]{1,2,0:T(8,128)(2,1)}), bf16[32,896,28]{1,2,0:T(8,128)(2,1)}, u32[]{:S(2)}, u32[]{:S(2)}) async-start(bf16[32,896,28]{1,2,0:T(8,128)(2,1)} %stack.8), calls=%async_computation.1 | async-start | bytes 3670016 | tf_op jit(solution)/shard_map/all_to_all | solution.py:70
  28.2 1.7 fusion.5
  29.9 163.1 %all-gather.7.cloned.1.call-done = bf16[32,28,896]{2,1,0:T(8,128)(2,1)} async-done(((bf16[1,28,896]{2,1,0:T(8,128)(2,1)}), bf16[32,28,896]{2,1,0:T(8,128)(2,1)}) %all-gather.7.cloned.1.call-update) | async-done | bytes 1605648 | tf_op jit(solution)/shard_map/all_gather | solution.py:88
  193.0 2.4 reshape.115
  195.5 3.6 reshape.109
  199.1 14.2 %fusion.23 = f32[1024,896]{1,0:T(8,128)} fusion(bf16[896,896]{0,1:T(8,128)(2,1)} %reshape.109, bf16[1024,896]{1,0:T(8,128)(2,1)} %fusion.5, bf16[896,896]{1,0:T(8,128)(2,1)S(1)} %reshape.115), kind=kOutput, calls=%fused_computation.41 | convolution fusion | flops 3347972096 | bytes 8716288 | tf_op jit(solution)/shard_map/dot_general | solution.py:91
  215.7 3.2 all-to-all-start
  218.9 87.4 %all-reduce.2.cloned.1.call-done = f32[1024,896]{1,0:T(8,128)} async-done(((f32[1024,896]{1,0:T(8,128)}), f32[1024,896]{1,0:T(8,128)}) %all-reduce.2.cloned.1.call-update) | async-done | bytes 3670032 | tf_op jit(solution)/shard_map/psum | solution.py:92
  306.3 2.4 fusion.6
  308.7 2.8 convolution_convert_fusion
  311.5 2.4 copy.32
  314.0 5.1 all-to-all-start.2
  319.4 141.0 %all-gather.9.cloned.1.call-done = bf16[32,28,1024]{2,1,0:T(8,128)(2,1)} async-done(((bf16[1,28,1024]{2,1,0:T(8,128)(2,1)}), bf16[32,28,1024]{2,1,0:T(8,128)(2,1)}) %all-gather.9.cloned.1.call-update) | async-done | bytes 1835024 | tf_op jit(solution)/shard_map/all_gather | solution.py:107
  460.4 3.8 reshape.117
  464.2 143.3 %all-gather.11.cloned.1.call-done = bf16[32,28,1024]{2,1,0:T(8,128)(2,1)} async-done(((bf16[1,28,1024]{2,1,0:T(8,128)(2,1)}), bf16[32,28,1024]{2,1,0:T(8,128)(2,1)}) %all-gather.11.cloned.1.call-update) | async-done | bytes 1835024 | tf_op jit(solution)/shard_map/all_gather | solution.py:103
  607.5 3.7 reshape.119
  611.2 4.6 fusion.25
  616.0 2.3 convert_bitcast_fusion.1
  619.9 2.3 convert_bitcast_fusion
  622.9 0.9 bitcast_reduce_fusion
  623.8 0.9 fusion.28
  624.8 1.0 fusion.36
  626.1 0.9 copy.67
  (50 shorter events, 6.7 us)
Async XLA Ops:
  6.5 21.2 %copy-start = (bf16[4,256,896]{2,1,0:T(8,128)(2,1)S(1)}, bf16[4,256,896]{2,1,0:T(8,128)(2,1)}, u32[]{:S(2)}) copy-start(bf16[4,256,896]{2,1,0:T(8,128)(2,1)} %param.9) | copy-start | bytes 5505028
  6.5 21.6 %copy-start.4 = (f32[896]{0:T(1024)S(1)}, f32[896]{0:T(1024)}, u32[]{:S(2)}) copy-start(f32[896]{0:T(1024)} %param.12) | copy-start | bytes 10756
  8.9 186.6 %all-to-all-start.1 = ((bf16[32,896,28]{1,2,0:T(8,128)(2,1)}), bf16[32,896,28]{1,2,0:T(8,128)(2,1)}, u32[]{:S(2)}, u32[]{:S(2)}) async-start(bf16[32,896,28]{1,2,0:T(8,128)(2,1)} %stack.8), calls=%async_computation.1 | async-start | bytes 3670016 | tf_op jit(solution)/shard_map/all_to_all | solution.py:70
  26.9 166.1 %all-gather.7.cloned.1.call-start = ((), (), s32[]{:S(2)}) async-start(), calls=%async_computation.4 | async-start | bytes 1892352 | tf_op jit(solution)/shard_map/all_gather | solution.py:88
  27.7 278.7 %all-reduce.2.cloned.1.call-start = ((), (), s32[]{:S(2)}) async-start(), calls=%async_computation.3 | async-start | bytes 7340032 | tf_op jit(solution)/shard_map/psum | solution.py:92
  213.2 1.3 copy-start.6
  213.2 1.6 copy-start.5
  213.3 247.2 %all-gather.9.cloned.1.call-start = ((), (), s32[]{:S(2)}) async-start(), calls=%async_computation.5 | async-start | bytes 2162688 | tf_op jit(solution)/shard_map/all_gather | solution.py:107
  214.0 393.5 %all-gather.11.cloned.1.call-start = ((), (), s32[]{:S(2)}) async-start(), calls=%async_computation.6 | async-start | bytes 2162688 | tf_op jit(solution)/shard_map/all_gather | solution.py:103
  215.7 98.3 %all-to-all-start = ((s32[4,2,2]{1,2,0:T(2,128)}), s32[4,2,2]{1,2,0:T(2,128)S(1)}, u32[]{:S(2)}, u32[]{:S(2)}) async-start(s32[4,2,2]{1,2,0:T(2,128)} %copy.29), calls=%async_computation | async-start | bytes 8192 | tf_op jit(solution)/shard_map/all_to_all | solution.py:97
  314.0 5.1 copy-start.3
  314.0 297.2 %all-to-all-start.2 = ((bf16[8,256,896]{2,1,0:T(8,128)(2,1)}), bf16[8,256,896]{2,1,0:T(8,128)(2,1)}, u32[]{:S(2)}, u32[]{:S(2)}) async-start(bf16[8,256,896]{2,1,0:T(8,128)(2,1)} %copy.32), calls=%async_computation.2 | async-start | bytes 7340032 | tf_op jit(solution)/shard_map/all_to_all | solution.py:96
  611.2 4.8 copy-start.1
  618.4 1.5 copy-start.2
Sparse Core Ops, SparseCore 0:
  30.8 162.1 all-gather.6
  213.4 92.9 all-reduce.1
  309.4 150.9 all-gather.8
  463.4 144.0 all-gather.10
